TPU v7x, 32 devices: a whole 2x2x4 slice. The times are simulated.
32 devices in a mesh: tgt: 8 (over z, core), src: 4 (over y, x).
Axes of the slice: x: 2, y: 2, z: 4, core: 2. Of those that a mesh axis runs over, the one named last changes fastest.
Arguments:
- right_side: float32 [8192], P(('tgt', 'src')), may hold values from -50 to 50
- targets: float32 [3, 8192], P(None, ('tgt', 'src')), may hold values from -1 to 1
- source_nodes: float32 [3, 16, 8192], P(None, None, ('tgt', 'src')), may hold values from -1 to 1
- node_weights: float32 [16, 8192], P(None, ('tgt', 'src')), may hold values from -0.02734375 to 0.02734375
- near_list: int32 [2, 384], P(None, ('tgt', 'src')), may hold values from 0 to 31, as said below
- near_count: int32 [32], P(('tgt', 'src')), may hold values from 1 to 12, as said below
- row_basis: float32 [32, 32, 256], P(('tgt', 'src')), may hold values from -1 to 1
- column_basis: float32 [32, 32, 256], P(('tgt', 'src')), may hold values from -0.375 to 0.375
- coupling: float32 [8, 4, 8, 4, 1024], P('tgt', None, None, 'src'), may hold values from -0.109375 to 0.109375
Outputs:
- solution: float32 [8192], P(('tgt', 'src'))
Inputs may be any that keep to these rules, and one draw needn't show every extreme that they name: `near_list`: for the device with tgt index i and src index j (slots j + i * 4 times 12 onward), every slot names a target cluster c with c // 4 = i and a source cluster d with d % 4 = j; the slots of one device name distinct pairs. `near_count`: some device has all 12 slots live.
All inputs are finite; a program needn't handle non-finite values.
Results may differ from a plain program's by a relative error of at most 0.0003.
Values sent between devices are 32-bit elements; how exact they have to be, the bound alone decides.
No kernel may reach another device: no remote copies, remote signals or barrier semaphores. Data moves between devices by JAX's collectives and lax.ppermute only.
A program may use at most 64 MiB of HBM per device.

v0:
```python
import jax
import jax.numpy as jnp
from jax import lax
from jax.sharding import PartitionSpec as P

spread_sq = 0.0004
norm_floor = 1e-06
highest = lax.Precision.HIGHEST


def tile_values(points, src_nodes, src_weights):
    summed = jnp.zeros((points.shape[1], src_nodes.shape[2]), jnp.float32)
    for node_index in range(src_nodes.shape[1]):
        offset_first = points[0][:, None] - src_nodes[0, node_index][None, :]
        offset_second = points[1][:, None] - src_nodes[1, node_index][None, :]
        offset_third = points[2][:, None] - src_nodes[2, node_index][None, :]
        distance = jnp.sqrt(
            offset_first * offset_first
            + offset_second * offset_second
            + offset_third * offset_third
            + spread_sq
        )
        summed = summed + src_weights[node_index][None, :] / distance
    return summed


def global_sum(value):
    return lax.psum(value, ("tgt", "src"))


def per_device(
    right_side,
    targets,
    source_nodes,
    node_weights,
    near_list,
    near_count,
    row_basis,
    column_basis,
    coupling,
):
    src_count = lax.axis_size("src")
    tgt_count = lax.axis_size("tgt")
    tgt_index = lax.axis_index("tgt")
    leaf_size = right_side.shape[0]
    slot_total = near_list.shape[1]
    rank_size = row_basis.shape[1]
    slot_ids = jnp.arange(slot_total, dtype=jnp.int32)
    live_slot = slot_ids < near_count[0]
    row_local = near_list[0] - tgt_index * src_count
    column_local = near_list[1] // src_count
    row_hits = (
        (row_local[:, None] == jnp.arange(src_count, dtype=jnp.int32)[None, :]) & live_slot[:, None]
    ).astype(jnp.float32)
    column_hits = (column_local[:, None] == jnp.arange(tgt_count, dtype=jnp.int32)[None, :]).astype(
        jnp.float32
    )
    near_mask = jnp.einsum("ka,kb->ab", row_hits, column_hits, precision=highest)
    coupled = (
        coupling.reshape(src_count, tgt_count, rank_size, rank_size)
        * (1.0 - near_mask)[:, :, None, None]
    )
    row_points = lax.all_gather(targets, "src", axis=1, tiled=True)
    row_blocks = row_points.reshape(3, src_count, leaf_size)
    row_bases = lax.all_gather(row_basis, "src", axis=0, tiled=True)
    node_rows, weight_rows = (
        lax.all_gather(source_nodes[None], "tgt", axis=0, tiled=True),
        lax.all_gather(node_weights[None], "tgt", axis=0, tiled=True),
    )

    def make_tile(slot_number):

        def compute(unused):
            return tile_values(
                row_blocks[:, row_local[slot_number]],
                node_rows[column_local[slot_number]],
                weight_rows[column_local[slot_number]],
            )

        def nothing(unused):
            return jnp.zeros((leaf_size, leaf_size), jnp.float32)

        return lax.cond(live_slot[slot_number], compute, nothing, 0)

    tile_cache = lax.map(make_tile, slot_ids)

    def operate(vector):
        coeffs = jnp.dot(column_basis[0], vector, precision=highest)
        value_rows, coeff_rows = (
            lax.all_gather(vector[None], "tgt", axis=0, tiled=True),
            lax.all_gather(coeffs[None], "tgt", axis=0, tiled=True),
        )
        selected = value_rows[column_local]
        contrib = jnp.einsum("kij,kj->ki", tile_cache, selected, precision=highest)
        near_rows = jnp.einsum("ka,ki->ai", row_hits, contrib, precision=highest)
        far_rows = jnp.einsum("abrs,bs->ar", coupled, coeff_rows, precision=highest)
        partial_rows = near_rows + jnp.einsum("ar,arp->ap", far_rows, row_bases, precision=highest)
        own_rows = lax.psum_scatter(partial_rows, "src", scatter_dimension=0, tiled=True)
        result = own_rows[0]
        return 0.5 * vector + result

    rhs_norm = jnp.sqrt(global_sum(jnp.sum(right_side * right_side)) + norm_floor)
    basis_one = right_side / rhs_norm
    image_one = operate(basis_one)
    proj_first = global_sum(jnp.sum(basis_one * image_one))
    rest_one = image_one - proj_first * basis_one
    height_first = jnp.sqrt(global_sum(jnp.sum(rest_one * rest_one)) + norm_floor)
    basis_two = rest_one / height_first
    image_two = operate(basis_two)
    proj_cross = global_sum(jnp.sum(basis_one * image_two))
    rest_two = image_two - proj_cross * basis_one
    proj_second = global_sum(jnp.sum(basis_two * rest_two))
    rest_two = rest_two - proj_second * basis_two
    height_second = jnp.sqrt(global_sum(jnp.sum(rest_two * rest_two)) + norm_floor)
    radius_first = jnp.sqrt(proj_first * proj_first + height_first * height_first)
    cos_first = proj_first / radius_first
    sin_first = height_first / radius_first
    rotated_top = cos_first * proj_cross + sin_first * proj_second
    rotated_low = cos_first * proj_second - sin_first * proj_cross
    radius_second = jnp.sqrt(rotated_low * rotated_low + height_second * height_second)
    coeff_second = -sin_first * rhs_norm * (rotated_low / radius_second) / radius_second
    coeff_first = (cos_first * rhs_norm - rotated_top * coeff_second) / radius_first
    return coeff_first * basis_one + coeff_second * basis_two


def solution(mesh):
    return jax.shard_map(
        per_device,
        mesh=mesh,
        in_specs=(
            P(("tgt", "src")),
            P(None, ("tgt", "src")),
            P(None, None, ("tgt", "src")),
            P(None, ("tgt", "src")),
            P(None, ("tgt", "src")),
            P(("tgt", "src")),
            P(("tgt", "src"), None, None),
            P(("tgt", "src"), None, None),
            P("tgt", None, None, "src", None),
        ),
        out_specs=P(("tgt", "src")),
        check_vma=False,
    )
```

profile of v0, /device:TPU:0, one launch (start us, length us, event | category | flops | bytes accessed | tf_op | source)
XLA Modules:
  0.0 570.8 jit_solution(8423042894770920571)
XLA Ops:
  1.4 17.0 %all-gather = f32[128,256]{1,0:T(8,128)} all-gather(f32[16,256]{1,0:T(8,128)} %param.16), channel_id=2, replica_groups=mesh['tgt'=8,'src'=4] {'tgt'}, dimensions={0}, use_global_device_ids=true | all-gather | bytes 147456 | tf_op jit(solution)/shard_map/all_gather | solution.py:68
  19.1 8.3 %all_gather.25 = f32[3,1024]{1,0:T(4,128)S(1)} all-gather(f32[3,256]{1,0:T(4,128)} %param.14), channel_id=1, replica_groups=mesh['tgt'=8,'src'=4] {'src'}, dimensions={1}, use_global_device_ids=true | all-gather | bytes 15360 | tf_op jit(solution)/shard_map/all_gather | solution.py:63
  27.4 15.8 %all-gather.1 = f32[24,16,256]{2,1,0:T(8,128)} all-gather(f32[3,16,256]{2,1,0:T(8,128)} %param.15), channel_id=3, replica_groups=mesh['tgt'=8,'src'=4] {'tgt'}, dimensions={0}, use_global_device_ids=true | all-gather | bytes 442368 | tf_op jit(solution)/shard_map/all_gather | solution.py:67
  43.2 71.8 %while.10 = (s32[]{:T(128)}, f32[12,256,256]{2,1,0:T(8,128)S(1)}, s32[12]{0:T(128)S(1)}, pred[12]{0:T(512)(128)(4,1)S(1)}, s32[12]{0:T(128)S(1)}, /*index=5*/f32...) while((s32[]{:T(128)}, f32[12,256,256]{2,1,0:T(8,128)S(1)}, ...), condition=%wide.region_5.6_spmd, body=%wide.region_2.0_spmd.sunk | while | flops 11468830 | bytes 1091180 | solution.py:85
  47.3 11.1 %conditional.2 = (f32[1,256,256]{2,1,0:T(8,128)S(1)}) conditional(s32[]{:T(128)} %bitcast.164, () %tuple.106, (s32[]{:T(128)}, s32[12]{0:T(128)S(1)}, f32[8,16,256]{2,1,0:T(8,128)}, s32[12]{0:T(128)S(1)}, f32[3,4,256]{2,1,0:T(4,128)S(1)}, /*index=5*/f32[8,3,16,256]{3,2,1,0:T(8,128)}) %tuple.107), branch_computations={%region_3.3_spmd, %region_4.4_spmd} | conditional | flops 11468824 | bytes 566658 | solution.py:83
  62.5 11.1 %conditional.2 = (f32[1,256,256]{2,1,0:T(8,128)S(1)}) conditional(s32[]{:T(128)} %bitcast.164, () %tuple.106, (s32[]{:T(128)}, s32[12]{0:T(128)S(1)}, f32[8,16,256]{2,1,0:T(8,128)}, s32[12]{0:T(128)S(1)}, f32[3,4,256]{2,1,0:T(4,128)S(1)}, /*index=5*/f32[8,3,16,256]{3,2,1,0:T(8,128)}) %tuple.107), branch_computations={%region_3.3_spmd, %region_4.4_spmd} | conditional | flops 11468824 | bytes 566658 | solution.py:83
  115.7 148.2 %psum.42 = f32[]{:T(128)} all-reduce(f32[]{:T(128)} %multiply_reduce_fusion.5), channel_id=1, replica_groups=mesh['tgt'=8,'src'=4] {'tgt','src'}, use_global_device_ids=true, to_apply=%region_1.2 | all-reduce | flops 1 | bytes 8 | tf_op jit(solution)/shard_map/psum | solution.py:28
  264.7 10.7 %all-gather.6 = f32[8,1,256]{2,1,0:T(1,128)S(1)} all-gather(f32[1,1,256]{2,1,0:T(1,128)S(1)} %bitcast.249), channel_id=4, replica_groups=mesh['tgt'=8,'src'=4] {'tgt'}, dimensions={0}, use_global_device_ids=true | all-gather | bytes 9216 | tf_op jit(solution)/shard_map/all_gather | solution.py:90
  276.0 2.7 fusion.12
  280.4 13.9 %all-reduce = f32[256]{0:T(256)S(1)} all-reduce(f32[256]{0:T(256)S(1)} %dynamic-update-slice), channel_id=5, replica_groups=mesh['tgt'=8,'src'=4] {'tgt'}, use_global_device_ids=true, to_apply=%add | all-reduce | flops 256 | bytes 2048
  295.9 2.2 convolution_bitcast_fusion.1
  298.1 9.4 %all_gather.29 = f32[4,32,256]{2,1,0:T(8,128)S(1)} all-gather(f32[1,32,256]{2,1,0:T(8,128)S(1)} %copy-done.3), channel_id=1, replica_groups=mesh['tgt'=8,'src'=4] {'src'}, dimensions={0}, use_global_device_ids=true | all-gather | bytes 163840 | tf_op jit(solution)/shard_map/all_gather | solution.py:65
  308.0 9.2 %all-reduce.2 = f32[4,256]{1,0:T(4,128)S(1)} all-reduce(f32[4,256]{1,0:T(4,128)S(1)} %convolution_add_fusion.1), channel_id=8, replica_groups=mesh['tgt'=8,'src'=4] {'src'}, use_global_device_ids=true, to_apply=%region_6.7.clone | all-reduce | flops 1024 | bytes 8192
  319.2 37.0 %psum.43 = f32[]{:T(128)} all-reduce(f32[]{:T(128)} %multiply_reduce_fusion.4), channel_id=1, replica_groups=mesh['tgt'=8,'src'=4] {'tgt','src'}, use_global_device_ids=true, to_apply=%region_8.9 | all-reduce | flops 1 | bytes 8 | tf_op jit(solution)/shard_map/psum | solution.py:28
  357.4 42.6 %psum.44 = f32[]{:T(128)} all-reduce(f32[]{:T(128)} %multiply_reduce_fusion.3), channel_id=1, replica_groups=mesh['tgt'=8,'src'=4] {'tgt','src'}, use_global_device_ids=true, to_apply=%region_10.11 | all-reduce | flops 1 | bytes 8 | tf_op jit(solution)/shard_map/psum | solution.py:28
  403.1 10.1 %all-gather.7 = f32[8,1,256]{2,1,0:T(1,128)S(1)} all-gather(f32[1,1,256]{2,1,0:T(1,128)S(1)} %bitcast.172), channel_id=6, replica_groups=mesh['tgt'=8,'src'=4] {'tgt'}, dimensions={0}, use_global_device_ids=true | all-gather | bytes 9216 | tf_op jit(solution)/shard_map/all_gather | solution.py:90
  413.8 2.7 fusion.10
  416.9 14.0 %all-reduce.1 = f32[256]{0:T(256)S(1)} all-reduce(f32[256]{0:T(256)S(1)} %dynamic-update-slice.1), channel_id=7, replica_groups=mesh['tgt'=8,'src'=4] {'tgt'}, use_global_device_ids=true, to_apply=%add.1 | all-reduce | flops 256 | bytes 2048
  431.0 2.2 convolution_bitcast_fusion
  433.7 10.0 %all-reduce.3 = f32[4,256]{1,0:T(4,128)S(1)} all-reduce(f32[4,256]{1,0:T(4,128)S(1)} %convolution_add_fusion), channel_id=9, replica_groups=mesh['tgt'=8,'src'=4] {'src'}, use_global_device_ids=true, to_apply=%region_11.12.clone | all-reduce | flops 1024 | bytes 8192
  445.0 37.0 %psum.45 = f32[]{:T(128)} all-reduce(f32[]{:T(128)} %multiply_reduce_fusion.2), channel_id=1, replica_groups=mesh['tgt'=8,'src'=4] {'tgt','src'}, use_global_device_ids=true, to_apply=%region_13.14 | all-reduce | flops 1 | bytes 8 | tf_op jit(solution)/shard_map/psum | solution.py:28
  483.3 42.4 %psum.46 = f32[]{:T(128)} all-reduce(f32[]{:T(128)} %multiply_reduce_fusion.1), channel_id=1, replica_groups=mesh['tgt'=8,'src'=4] {'tgt','src'}, use_global_device_ids=true, to_apply=%region_15.16 | all-reduce | flops 1 | bytes 8 | tf_op jit(solution)/shard_map/psum | solution.py:28
  527.1 1.9 multiply_reduce_fusion
  529.0 39.1 %psum.47 = f32[]{:T(128)} all-reduce(f32[]{:T(128)} %multiply_reduce_fusion), channel_id=1, replica_groups=mesh['tgt'=8,'src'=4] {'tgt','src'}, use_global_device_ids=true, to_apply=%region_17.18 | all-reduce | flops 1 | bytes 8 | tf_op jit(solution)/shard_map/psum | solution.py:28
  (125 shorter events, 41.3 us)
Async XLA Ops:
  0.0 278.7 %copy-start = (f32[1,32,256]{2,1,0:T(8,128)S(1)}, f32[1,32,256]{2,1,0:T(8,128)}, u32[]{:S(2)}) copy-start(f32[1,32,256]{2,1,0:T(8,128)} %param.20) | copy-start | bytes 98308
  43.2 71.9 %copy-start.2 = (f32[256]{0:T(256)S(1)}, f32[256]{0:T(256)}, u32[]{:S(2)}) copy-start(f32[256]{0:T(256)} %param.13) | copy-start | bytes 3076
  43.2 232.1 %copy-start.4 = (s32[2,12]{1,0:T(2,128)S(1)}, s32[2,12]{1,0:T(2,128)}, u32[]{:S(2)}) copy-start(s32[2,12]{1,0:T(2,128)} %param.17) | copy-start | bytes 292
  115.1 163.8 %copy-start.6 = (u32[32]{0:T(128)S(1)}, u32[32]{0:T(128)}, u32[]{:S(2)}) copy-start(u32[32]{0:T(128)} %constant.65) | copy-start | bytes 388
  115.1 179.3 %copy-start.1 = (f32[1,4,8,1,1024]{4,3,2,1,0:T(1,128)S(1)}, f32[1,4,8,1,1024]{4,3,2,1,0:T(1,128)}, u32[]{:S(2)}) copy-start(f32[1,4,8,1,1024]{4,3,2,1,0:T(1,128)} %param.21) | copy-start | bytes 393220
  115.1 183.0 %copy-start.3 = (f32[1,32,256]{2,1,0:T(8,128)S(1)}, f32[1,32,256]{2,1,0:T(8,128)}, u32[]{:S(2)}) copy-start(f32[1,32,256]{2,1,0:T(8,128)} %param.19) | copy-start | bytes 98308
  115.1 202.1 %copy-start.5 = (u32[32]{0:T(128)S(1)}, u32[32]{0:T(128)}, u32[]{:S(2)}) copy-start(u32[32]{0:T(128)} %constant.77) | copy-start | bytes 388
where the time goes:
time: 575 us; the launch traced here: 571 us
  blocking collectives  465 us (81%)
  loops' own time  45.1 us (8%)
  local copies, waits for them, and re-layouts  28.4 us (5%)
  other arithmetic  13 us (2%)
  matrix products  11.4 us (2%)
  between operations  8.12 us (1%)
    psum x6, blocking collectives, global_sum(): return lax.psum(value, ('tgt', 'src'))  346 us
    unnamed x4, blocking collectives  47.1 us
    another operation x1, loops' own time, per_device(): tile_cache = lax.map(make_tile, slot_ids)  33 us
    all_gather x2, blocking collectives, operate(): lax.all_gather(vector[None], 'tgt', axis=0, tiled=True)  20.8 us
    all_gather x1, blocking collectives, per_device(): lax.all_gather(node_weights[None], 'tgt', axis=0, tiled=True)  17 us
    all_gather x1, blocking collectives, per_device(): lax.all_gather(source_nodes[None], 'tgt', axis=0, tiled=True)  15.8 us
    another operation x12, loops' own time, make_tile(): return lax.cond(live_slot[slot_number], compute, nothing, 0)  12.1 us

commit v1 on v0

--- a/solution.py
+++ b/solution.py
@@ -6,6 +6,11 @@
 spread_sq = 0.0004
 norm_floor = 1e-06
 highest = lax.Precision.HIGHEST
+
+
+def one_after_other(value_2, one, other):
+    inner = lax.psum(value_2, one)
+    return lax.psum(inner, other)
 
 
 def tile_values(points, src_nodes, src_weights):
@@ -25,7 +30,7 @@
 
 
 def global_sum(value):
-    return lax.psum(value, ("tgt", "src"))
+    return one_after_other(value, "src", "tgt")
 
 
 def per_device(

time: 575 us -> 477 us (0.83)
  blocking collectives: 465 us -> 367 us
    psum x6 -> x12, blocking collectives: 346 us -> 252 us  [the longest x6 166 us: one_after_other(): inner = lax.psum(value_2, one)]
where the time goes in v1:
time: 477 us; the launch traced here: 473 us
  blocking collectives  367 us (77%)
  loops' own time  45.1 us (9%)
  local copies, waits for them, and re-layouts  28.4 us (6%)
  other arithmetic  13 us (3%)
  matrix products  11.4 us (2%)
  between operations  8.12 us (2%)
    psum x6, blocking collectives, one_after_other(): inner = lax.psum(value_2, one)  166 us
    psum x6, blocking collectives, one_after_other(): return lax.psum(inner, other)  85.4 us
    unnamed x4, blocking collectives  48.8 us
    another operation x1, loops' own time, per_device(): tile_cache = lax.map(make_tile, slot_ids)  33 us
    all_gather x1, blocking collectives, per_device(): lax.all_gather(node_weights[None], 'tgt', axis=0, tiled=True)  17 us
    all_gather x2, blocking collectives, operate(): lax.all_gather(vector[None], 'tgt', axis=0, tiled=True)  16.9 us
    all_gather x1, blocking collectives, per_device(): lax.all_gather(source_nodes[None], 'tgt', axis=0, tiled=True)  15.8 us
    another operation x12, loops' own time, make_tile(): return lax.cond(live_slot[slot_number], compute, nothing, 0)  12.1 us

profile of v1, /device:TPU:0, one launch (start us, length us, event | category | flops | bytes accessed | tf_op | source)
XLA Modules:
  0.0 472.8 jit_solution(10123783626653852580)
XLA Ops:
  1.4 17.0 %all-gather = f32[128,256]{1,0:T(8,128)} all-gather(f32[16,256]{1,0:T(8,128)} %param.16), channel_id=2, replica_groups=mesh['tgt'=8,'src'=4] {'tgt'}, dimensions={0}, use_global_device_ids=true | all-gather | bytes 147456 | tf_op jit(solution)/shard_map/all_gather | solution.py:73
  27.4 15.8 %all-gather.1 = f32[24,16,256]{2,1,0:T(8,128)} all-gather(f32[3,16,256]{2,1,0:T(8,128)} %param.15), channel_id=3, replica_groups=mesh['tgt'=8,'src'=4] {'tgt'}, dimensions={0}, use_global_device_ids=true | all-gather | bytes 442368 | tf_op jit(solution)/shard_map/all_gather | solution.py:72
  43.2 71.8 %while.10 = (s32[]{:T(128)}, f32[12,256,256]{2,1,0:T(8,128)S(1)}, s32[12]{0:T(128)S(1)}, pred[12]{0:T(512)(128)(4,1)S(1)}, s32[12]{0:T(128)S(1)}, /*index=5*/f32...) while((s32[]{:T(128)}, f32[12,256,256]{2,1,0:T(8,128)S(1)}, ...), condition=%wide.region_6.7_spmd, body=%wide.region_3.6_spmd.sunk | while | flops 11468830 | bytes 1091180 | solution.py:90
  47.3 11.1 %conditional.2 = (f32[1,256,256]{2,1,0:T(8,128)S(1)}) conditional(s32[]{:T(128)} %bitcast.164, () %tuple.106, (s32[]{:T(128)}, s32[12]{0:T(128)S(1)}, f32[8,16,256]{2,1,0:T(8,128)}, s32[12]{0:T(128)S(1)}, f32[3,4,256]{2,1,0:T(4,128)S(1)}, /*index=5*/f32[8,3,16,256]{3,2,1,0:T(8,128)}) %tuple.107), branch_computations={%region_4.4_spmd, %region_5.5_spmd} | conditional | flops 11468824 | bytes 566658 | solution.py:88
  62.5 11.1 %conditional.2 = (f32[1,256,256]{2,1,0:T(8,128)S(1)}) conditional(s32[]{:T(128)} %bitcast.164, () %tuple.106, (s32[]{:T(128)}, s32[12]{0:T(128)S(1)}, f32[8,16,256]{2,1,0:T(8,128)}, s32[12]{0:T(128)S(1)}, f32[3,4,256]{2,1,0:T(4,128)S(1)}, /*index=5*/f32[8,3,16,256]{3,2,1,0:T(8,128)}) %tuple.107), branch_computations={%region_4.4_spmd, %region_5.5_spmd} | conditional | flops 11468824 | bytes 566658 | solution.py:88
  115.7 120.3 %psum.84 = f32[]{:T(128)} all-reduce(f32[]{:T(128)} %multiply_reduce_fusion.5), channel_id=1, replica_groups=mesh['tgt'=8,'src'=4] {'src'}, use_global_device_ids=true, to_apply=%region_1.2 | all-reduce | flops 1 | bytes 8 | tf_op jit(solution)/shard_map/psum | solution.py:12
  236.1 14.2 %psum.85 = f32[]{:T(128)} all-reduce(f32[]{:T(128)} %psum.84), channel_id=1, replica_groups=mesh['tgt'=8,'src'=4] {'tgt'}, use_global_device_ids=true, to_apply=%region_2.3 | all-reduce | flops 1 | bytes 8 | tf_op jit(solution)/shard_map/psum | solution.py:13
  251.0 8.4 %all-gather.6 = f32[8,1,256]{2,1,0:T(1,128)S(1)} all-gather(f32[1,1,256]{2,1,0:T(1,128)S(1)} %bitcast.249), channel_id=4, replica_groups=mesh['tgt'=8,'src'=4] {'tgt'}, dimensions={0}, use_global_device_ids=true | all-gather | bytes 9216 | tf_op jit(solution)/shard_map/all_gather | solution.py:95
  264.4 15.5 %all-reduce = f32[256]{0:T(256)S(1)} all-reduce(f32[256]{0:T(256)S(1)} %dynamic-update-slice), channel_id=5, replica_groups=mesh['tgt'=8,'src'=4] {'tgt'}, use_global_device_ids=true, to_apply=%add | all-reduce | flops 256 | bytes 2048
  283.8 8.4 %all_gather.29 = f32[4,32,256]{2,1,0:T(8,128)S(1)} all-gather(f32[1,32,256]{2,1,0:T(8,128)S(1)} %copy-done.3), channel_id=1, replica_groups=mesh['tgt'=8,'src'=4] {'src'}, dimensions={0}, use_global_device_ids=true | all-gather | bytes 163840 | tf_op jit(solution)/shard_map/all_gather | solution.py:70
  292.6 8.9 %all-reduce.2 = f32[4,256]{1,0:T(4,128)S(1)} all-reduce(f32[4,256]{1,0:T(4,128)S(1)} %convolution_add_fusion.1), channel_id=8, replica_groups=mesh['tgt'=8,'src'=4] {'src'}, use_global_device_ids=true, to_apply=%region_7.8.clone | all-reduce | flops 1024 | bytes 8192
  303.5 8.6 %psum.86 = f32[]{:T(128)} all-reduce(f32[]{:T(128)} %multiply_reduce_fusion.4), channel_id=1, replica_groups=mesh['tgt'=8,'src'=4] {'src'}, use_global_device_ids=true, to_apply=%region_9.10 | all-reduce | flops 1 | bytes 8 | tf_op jit(solution)/shard_map/psum | solution.py:12
  312.1 14.2 %psum.87 = f32[]{:T(128)} all-reduce(f32[]{:T(128)} %psum.86), channel_id=1, replica_groups=mesh['tgt'=8,'src'=4] {'tgt'}, use_global_device_ids=true, to_apply=%region_10.11 | all-reduce | flops 1 | bytes 8 | tf_op jit(solution)/shard_map/psum | solution.py:13
  327.6 9.6 %psum.88 = f32[]{:T(128)} all-reduce(f32[]{:T(128)} %multiply_reduce_fusion.3), channel_id=1, replica_groups=mesh['tgt'=8,'src'=4] {'src'}, use_global_device_ids=true, to_apply=%region_12.13 | all-reduce | flops 1 | bytes 8 | tf_op jit(solution)/shard_map/psum | solution.py:12
  337.2 14.3 %psum.89 = f32[]{:T(128)} all-reduce(f32[]{:T(128)} %psum.88), channel_id=1, replica_groups=mesh['tgt'=8,'src'=4] {'tgt'}, use_global_device_ids=true, to_apply=%region_13.14 | all-reduce | flops 1 | bytes 8 | tf_op jit(solution)/shard_map/psum | solution.py:13
  354.5 8.4 %all-gather.7 = f32[8,1,256]{2,1,0:T(1,128)S(1)} all-gather(f32[1,1,256]{2,1,0:T(1,128)S(1)} %bitcast.172), channel_id=6, replica_groups=mesh['tgt'=8,'src'=4] {'tgt'}, dimensions={0}, use_global_device_ids=true | all-gather | bytes 9216 | tf_op jit(solution)/shard_map/all_gather | solution.py:95
  366.6 15.5 %all-reduce.1 = f32[256]{0:T(256)S(1)} all-reduce(f32[256]{0:T(256)S(1)} %dynamic-update-slice.1), channel_id=7, replica_groups=mesh['tgt'=8,'src'=4] {'tgt'}, use_global_device_ids=true, to_apply=%add.1 | all-reduce | flops 256 | bytes 2048
  384.9 8.9 %all-reduce.3 = f32[4,256]{1,0:T(4,128)S(1)} all-reduce(f32[4,256]{1,0:T(4,128)S(1)} %convolution_add_fusion), channel_id=9, replica_groups=mesh['tgt'=8,'src'=4] {'src'}, use_global_device_ids=true, to_apply=%region_14.15.clone | all-reduce | flops 1024 | bytes 8192
  395.1 9.5 %psum.90 = f32[]{:T(128)} all-reduce(f32[]{:T(128)} %multiply_reduce_fusion.2), channel_id=1, replica_groups=mesh['tgt'=8,'src'=4] {'src'}, use_global_device_ids=true, to_apply=%region_16.17 | all-reduce | flops 1 | bytes 8 | tf_op jit(solution)/shard_map/psum | solution.py:12
  404.6 14.2 %psum.91 = f32[]{:T(128)} all-reduce(f32[]{:T(128)} %psum.90), channel_id=1, replica_groups=mesh['tgt'=8,'src'=4] {'tgt'}, use_global_device_ids=true, to_apply=%region_17.18 | all-reduce | flops 1 | bytes 8 | tf_op jit(solution)/shard_map/psum | solution.py:13
  420.1 8.8 %psum.92 = f32[]{:T(128)} all-reduce(f32[]{:T(128)} %multiply_reduce_fusion.1), channel_id=1, replica_groups=mesh['tgt'=8,'src'=4] {'src'}, use_global_device_ids=true, to_apply=%region_19.20 | all-reduce | flops 1 | bytes 8 | tf_op jit(solution)/shard_map/psum | solution.py:12
  428.9 14.3 %psum.93 = f32[]{:T(128)} all-reduce(f32[]{:T(128)} %psum.92), channel_id=1, replica_groups=mesh['tgt'=8,'src'=4] {'tgt'}, use_global_device_ids=true, to_apply=%region_20.21 | all-reduce | flops 1 | bytes 8 | tf_op jit(solution)/shard_map/psum | solution.py:13
  446.5 9.4 %psum.94 = f32[]{:T(128)} all-reduce(f32[]{:T(128)} %multiply_reduce_fusion), channel_id=1, replica_groups=mesh['tgt'=8,'src'=4] {'src'}, use_global_device_ids=true, to_apply=%region_22.23 | all-reduce | flops 1 | bytes 8 | tf_op jit(solution)/shard_map/psum | solution.py:12
  455.9 14.2 %psum.95 = f32[]{:T(128)} all-reduce(f32[]{:T(128)} %psum.94), channel_id=1, replica_groups=mesh['tgt'=8,'src'=4] {'tgt'}, use_global_device_ids=true, to_apply=%region_23.24 | all-reduce | flops 1 | bytes 8 | tf_op jit(solution)/shard_map/psum | solution.py:13
  (131 shorter events, 61.5 us)
Async XLA Ops:
  0.0 262.8 %copy-start = (f32[1,32,256]{2,1,0:T(8,128)S(1)}, f32[1,32,256]{2,1,0:T(8,128)}, u32[]{:S(2)}) copy-start(f32[1,32,256]{2,1,0:T(8,128)} %param.20) | copy-start | bytes 98308
  43.2 71.9 %copy-start.2 = (f32[256]{0:T(256)S(1)}, f32[256]{0:T(256)}, u32[]{:S(2)}) copy-start(f32[256]{0:T(256)} %param.13) | copy-start | bytes 3076
  43.2 216.2 %copy-start.4 = (s32[2,12]{1,0:T(2,128)S(1)}, s32[2,12]{1,0:T(2,128)}, u32[]{:S(2)}) copy-start(s32[2,12]{1,0:T(2,128)} %param.17) | copy-start | bytes 292
  115.1 147.8 %copy-start.6 = (u32[32]{0:T(128)S(1)}, u32[32]{0:T(128)}, u32[]{:S(2)}) copy-start(u32[32]{0:T(128)} %constant.65) | copy-start | bytes 388
  115.1 164.9 %copy-start.1 = (f32[1,4,8,1,1024]{4,3,2,1,0:T(1,128)S(1)}, f32[1,4,8,1,1024]{4,3,2,1,0:T(1,128)}, u32[]{:S(2)}) copy-start(f32[1,4,8,1,1024]{4,3,2,1,0:T(1,128)} %param.21) | copy-start | bytes 393220
  115.1 168.7 %copy-start.3 = (f32[1,32,256]{2,1,0:T(8,128)S(1)}, f32[1,32,256]{2,1,0:T(8,128)}, u32[]{:S(2)}) copy-start(f32[1,32,256]{2,1,0:T(8,128)} %param.19) | copy-start | bytes 98308
  115.1 186.4 %copy-start.5 = (u32[32]{0:T(128)S(1)}, u32[32]{0:T(128)}, u32[]{:S(2)}) copy-start(u32[32]{0:T(128)} %constant.77) | copy-start | bytes 388
